TPU v7x, 1024 devices: a whole 4x8x16 slice. The times are simulated.
1024 devices in a mesh: lat: 64 (over z, x), azim: 16 (over y, core).
Axes of the slice: x: 4, y: 8, z: 16, core: 2. Of those that a mesh axis runs over, the one named last changes fastest.
Arguments:
- magnetic: float32 [3, 32, 2048, 2048], P(None, None, 'lat', 'azim'), may hold values from -6 to 6
- kept_modes: int32 [2048], replicated, may hold values from 1 to 1024, as said below
Outputs:
- current_density: float32 [3, 32, 2048, 2048], P(None, None, 'lat', 'azim')
Inputs may be any that keep to these rules, and one draw needn't show every extreme that they name: `kept_modes`: at latitude 2048 // 2 all 1024 modes are kept.
All inputs are finite; a program needn't handle non-finite values.
Results may differ from a plain program's by a relative error of at most 0.000068.
Values sent between devices are 32-bit elements; how exact they have to be, the bound alone decides.
A program may use at most 32 MiB of HBM per device.

v0:
```python
import functools
import math

import jax
import jax.numpy as jnp
import numpy as np
from jax import lax
from jax.experimental import pallas as pl
from jax.experimental.pallas import tpu as pltpu
from jax.sharding import PartitionSpec as P

MESH = pl.DeviceIdType.MESH
F32 = jnp.float32
BF16 = jnp.bfloat16

inner_radius = 0.7
stencil_coeffs = (-1.0 / 60.0, 3.0 / 20.0, -3.0 / 4.0, 0.0, 3.0 / 4.0, -3.0 / 20.0, 1.0 / 60.0)
OFFSETS = (-3, -2, -1, 1, 2, 3)

RAD = 32
BAND = 32
SEG = 128
AZ = 16
HALF = BAND // AZ
ROWS = 2 * RAD
PADR = 3 * BAND


def mode_tables():
    a = np.arange(128)[:, None]
    b = np.arange(32)[:, None]
    q = np.arange(SEG)[None, :]
    p = np.arange(AZ)[:, None]
    high = 2.0 * np.pi * ((a * q) % 64) / 64.0
    twist = 2.0 * np.pi * ((b * q) % 2048) / 2048.0
    low = 2.0 * np.pi * ((p * b.T) % 16) / 16.0
    first = np.concatenate([np.cos(high), np.sin(high)], axis=1)
    second = np.stack([np.cos(twist), np.sin(twist)])
    third = np.stack([np.cos(low), np.sin(low)])
    third = np.pad(third, ((0, 0), (0, 0), (0, 96)))
    return first.astype(np.float32), second.astype(np.float32), third.astype(np.float32)


def split(value):
    high = value.astype(BF16)
    return high, (value - high.astype(F32)).astype(BF16)


def send_order():
    order = []
    for chips in (4, 3, -3, 2, -2, 1, -1, 0):
        for core in (0, 1):
            order.append((chips, core))
    return order


def kernel(
    lat_total,
    x4, x3, kept_hbm, latsc_hbm, radsc_hbm, tab1, tab2, tab3,
    out,
    kept, latsc, radsc, xs, ext, xt, rcv, whi, wlo, fhi, flo, acc, ret, az, outv, cot, gen,
    in_sem, small_sem, fsend, frecv, rsend, rrecv, hsend, hrecv, out_sem,
):
    lat = lax.axis_index("lat")
    me = lax.axis_index("azim")
    lats = lax.axis_size("lat")
    chip = me // 2
    core = me % 2
    north = (lat + lats - 1) % lats
    south = (lat + 1) % lats

    loads = [
        pltpu.make_async_copy(x3.at[0:2], xs.at[:, PADR : PADR + RAD * BAND, :], in_sem.at[0]),
        pltpu.make_async_copy(x4.at[0], ext.at[0, 3 : 3 + RAD, 8 : 8 + BAND, :], in_sem.at[1]),
        pltpu.make_async_copy(x4.at[2], ext.at[1, 3 : 3 + RAD, 8 : 8 + BAND, :], in_sem.at[2]),
    ]
    smalls = [
        pltpu.make_async_copy(kept_hbm, kept, small_sem.at[0]),
        pltpu.make_async_copy(latsc_hbm, latsc, small_sem.at[1]),
        pltpu.make_async_copy(radsc_hbm, radsc, small_sem.at[2]),
    ]
    for copy in loads + smalls:
        copy.start()

    barrier = pltpu.get_barrier_semaphore()
    for step in range(1, AZ):
        pl.semaphore_signal(barrier, inc=1, device_id={"azim": (me + step) % AZ}, device_id_type=MESH)
    pl.semaphore_signal(barrier, inc=1, device_id={"lat": north}, device_id_type=MESH)
    pl.semaphore_signal(barrier, inc=1, device_id={"lat": south}, device_id_type=MESH)
    loads[0].wait()
    pl.semaphore_wait(barrier, AZ + 1)

    peers = []
    for chips, flip in send_order():
        peer = ((chip + chips + 8) % 8) * 2 + (core + flip) % 2
        peers.append((peer, chips == 0 and flip == 0))
    forward = []
    for half in range(HALF):
        for peer, own in peers:
            row = peer + AZ * half
            for c in range(2):
                for k in range(RAD // 8):
                    xt[row, c * RAD + 8 * k : c * RAD + 8 * k + 8, :] = xs[
                        c, pl.ds(PADR + 8 * k * BAND + row, 8, stride=BAND), :
                    ]
            if own:
                pltpu.make_async_copy(xt.at[row], rcv.at[half, me], frecv.at[half, me]).start()
            else:
                copy = pltpu.make_async_remote_copy(
                    src_ref=xt.at[row],
                    dst_ref=rcv.at[half, me],
                    send_sem=fsend.at[half, peer],
                    recv_sem=frecv.at[half, me],
                    device_id={"azim": peer},
                    device_id_type=MESH,
                )
                copy.start()
                forward.append(copy)

    loads[1].wait()
    loads[2].wait()
    halos = [
        pltpu.make_async_remote_copy(
            src_ref=ext.at[:, 3 : 3 + RAD, BAND : BAND + 8, :],
            dst_ref=ext.at[:, 3 : 3 + RAD, 0:8, :],
            send_sem=hsend.at[0],
            recv_sem=hrecv.at[0],
            device_id={"lat": south},
            device_id_type=MESH,
        ),
        pltpu.make_async_remote_copy(
            src_ref=ext.at[:, 3 : 3 + RAD, 8:16, :],
            dst_ref=ext.at[:, 3 : 3 + RAD, 8 + BAND : 16 + BAND, :],
            send_sem=hsend.at[1],
            recv_sem=hrecv.at[1],
            device_id={"lat": north},
            device_id_type=MESH,
        ),
    ]
    for copy in halos:
        copy.start()
    for copy in smalls:
        copy.wait()

    base = lat * BAND + me
    side = lax.broadcasted_iota(jnp.int32, (HALF * 32, 128), 0)
    a = lax.broadcasted_iota(jnp.int32, (HALF * 32, 128), 1)
    mode = 32 * a + side % 32
    first_half = side < 32
    limit = jnp.where(first_half, kept[base], kept[base + AZ])
    scale = jnp.where(first_half, latsc[base], latsc[base + AZ])
    weight = jnp.where(mode < limit, mode, 0).astype(F32) * (2.0 / (AZ * SEG)) * scale
    sums = jnp.dot(weight, tab1[...], precision=lax.Precision.HIGHEST, preferred_element_type=F32)
    for half in range(HALF):
        c_sum = sums[32 * half : 32 * half + 32, 0:SEG]
        s_sum = sums[32 * half : 32 * half + 32, SEG : 2 * SEG]
        tc = tab2[0]
        ts = tab2[1]
        zero = jnp.zeros((96, SEG), F32)
        real = jnp.concatenate([c_sum * tc - s_sum * ts, zero], axis=0)
        imag = jnp.concatenate([s_sum * tc + c_sum * ts, zero], axis=0)
        gen[half] = -(
            jnp.dot(tab3[0], imag, precision=lax.Precision.HIGHEST, preferred_element_type=F32)
            + jnp.dot(tab3[1], real, precision=lax.Precision.HIGHEST, preferred_element_type=F32)
        )
    for half in range(HALF):
        for p in range(AZ):
            pair = jnp.concatenate(
                [gen[half, (p + AZ - 1) % AZ : (p + AZ - 1) % AZ + 1, :], gen[half, p : p + 1, :]], axis=1
            )
            turned = pltpu.roll(jnp.broadcast_to(pair, (SEG, 2 * SEG)), 0, 1, stride=1, stride_axis=0)
            high, low = split(turned[:, SEG:])
            for tile in range(8):
                for i in range(2):
                    for j in range(2):
                        if (j - i - 2 * tile - p) % AZ == 0:
                            at = (half, tile, slice(SEG * i, SEG * i + SEG), slice(SEG * j, SEG * j + SEG))
                            whi[at] = high
                            wlo[at] = low

    zeros = jnp.zeros((3, BAND, SEG), F32)
    ext[1, 0:3, 8 : 8 + BAND, :] = zeros
    ext[1, 3 + RAD : 6 + RAD, 8 : 8 + BAND, :] = zeros
    xs[1, 0:PADR, :] = jnp.zeros((PADR, SEG), F32)
    xs[1, PADR + RAD * BAND : 2 * PADR + RAD * BAND, :] = jnp.zeros((PADR, SEG), F32)
    for t in range(BAND):
        cot[t : t + 1, :] = jnp.full((1, SEG), latsc[lat_total + lat * BAND + t], F32)
    for copy in halos:
        copy.wait_recv()

    def stencils(r, carry):
        for c in range(2):
            top = ext[c, r + 3, 0:8, :]
            ext[c, r + 3, 0:8, :] = jnp.where(lat == 0, jnp.zeros_like(top), top)
            end = ext[c, r + 3, 8 + BAND : 16 + BAND, :]
            ext[c, r + 3, 8 + BAND : 16 + BAND, :] = jnp.where(lat == lats - 1, jnp.zeros_like(end), end)
        inverse = radsc[64 + r]
        th_r = jnp.zeros((BAND, SEG), F32)
        th_p = jnp.zeros((BAND, SEG), F32)
        dr_t = jnp.zeros((BAND, SEG), F32)
        dr_p = jnp.zeros((BAND, SEG), F32)
        for o in OFFSETS:
            weight_o = stencil_coeffs[o + 3]
            th_r = th_r + weight_o * ext[0, r + 3, 8 + o : 8 + o + BAND, :]
            th_p = th_p + weight_o * ext[1, r + 3, 8 + o : 8 + o + BAND, :]
            scaled = weight_o * radsc[r + 3 + o]
            dr_t = dr_t + scaled * xs[1, pl.ds(pl.multiple_of((r + 3 + o) * BAND, BAND), BAND), :]
            dr_p = dr_p + scaled * ext[1, r + 3 + o, 8 : 8 + BAND, :]
        outv[0, r] = (th_p + cot[...] * ext[1, r + 3, 8 : 8 + BAND, :]) * inverse
        outv[1, r] = -dr_p * inverse
        outv[2, r] = (dr_t - th_r) * inverse
        return carry

    def convert_and_apply(half):
        for source in range(AZ):
            pltpu.make_async_copy(xt.at[0], rcv.at[half, source], frecv.at[half, source]).wait()
        for source in range(AZ):
            high, low = split(rcv[half, source])
            lanes = slice(SEG * (source % 2), SEG * (source % 2) + SEG)
            for wrap in range(2):
                rows = slice(ROWS * (source // 2 + 8 * wrap), ROWS * (source // 2 + 8 * wrap) + ROWS)
                fhi[rows, lanes] = high
                flo[rows, lanes] = low
        acc[...] = jnp.zeros_like(acc)

        def tile_step(tile, carry):
            rows = pl.ds(pl.multiple_of(tile * ROWS, ROWS), 8 * ROWS)
            f_high = fhi[rows, :]
            f_low = flo[rows, :]
            w_high = whi[half, tile]
            acc[...] += (
                jnp.dot(f_high, w_high, preferred_element_type=F32)
                + jnp.dot(f_high, wlo[half, tile], preferred_element_type=F32)
                + jnp.dot(f_low, w_high, preferred_element_type=F32)
            )
            return carry

        lax.fori_loop(0, 8, tile_step, 0)
        for block in range(AZ):
            ret[half, block] = acc[
                ROWS * (block // 2) : ROWS * (block // 2) + ROWS, SEG * (block % 2) : SEG * (block % 2) + SEG
            ]
        sent = []
        for peer, own in peers:
            target = az.at[pl.ds(pl.multiple_of((me + AZ * half) * ROWS, ROWS), ROWS), :]
            if own:
                pltpu.make_async_copy(ret.at[half, peer], target, rrecv.at[half, me]).start()
            else:
                copy = pltpu.make_async_remote_copy(
                    src_ref=ret.at[half, peer],
                    dst_ref=target,
                    send_sem=rsend.at[half, peer],
                    recv_sem=rrecv.at[half, me],
                    device_id={"azim": peer},
                    device_id_type=MESH,
                )
                copy.start()
                sent.append(copy)
        return sent

    def finish(half):
        for source in range(AZ):
            t = source + AZ * half
            pltpu.make_async_copy(
                ret.at[half, 0], az.at[t * ROWS : t * ROWS + ROWS, :], rrecv.at[half, source]
            ).wait()

        def combine(r, carry):
            inverse = radsc[64 + r]
            for k in range(AZ // 8):
                t = AZ * half + 8 * k
                azim_r = az[pl.ds(t * ROWS + r, 8, stride=ROWS), :]
                azim_t = az[pl.ds(t * ROWS + RAD + r, 8, stride=ROWS), :]
                outv[0, r, t : t + 8, :] = outv[0, r, t : t + 8, :] - azim_t * inverse
                outv[1, r, t : t + 8, :] = outv[1, r, t : t + 8, :] + azim_r * inverse
            return carry

        lax.fori_loop(0, RAD, combine, 0)
        where = (slice(0, 2), slice(None), slice(AZ * half, AZ * half + AZ), slice(None))
        copy = pltpu.make_async_copy(outv.at[where], out.at[where], out_sem.at[half])
        copy.start()
        return copy

    lax.fori_loop(0, RAD, stencils, 0)
    written = [pltpu.make_async_copy(outv.at[2], out.at[2], out_sem.at[2])]
    written[0].start()
    back = []
    for half in range(HALF):
        back += convert_and_apply(half)
    for half in range(HALF):
        written.append(finish(half))
    for copy in forward + back + halos:
        copy.wait_send()
    for copy in written:
        copy.wait()


def solution(mesh):
    lat_total = BAND * mesh.shape["lat"]
    spacing = math.pi / lat_total
    theta = (np.arange(lat_total, dtype=np.float32) + np.float32(0.5)) * np.float32(spacing)
    theta = theta.astype(np.float64)
    lat_scalars = np.concatenate([spacing / np.sin(theta), spacing * np.cos(theta) / np.sin(theta)]).astype(np.float32)
    radius = inner_radius + (np.arange(RAD) + 0.5) * spacing
    rad_scalars = np.zeros(128, np.float32)
    rad_scalars[3 : 3 + RAD] = radius
    rad_scalars[64 : 64 + RAD] = 1.0 / radius
    first, second, third = mode_tables()

    def on_device(magnetic, kept_modes):
        flat = magnetic.reshape(3, RAD * BAND, SEG)
        anywhere = pl.BlockSpec(memory_space=pl.ANY)
        in_vmem = pl.BlockSpec(memory_space=pltpu.VMEM)
        dma = pltpu.SemaphoreType.DMA
        return pl.pallas_call(
            functools.partial(kernel, lat_total),
            out_shape=jax.ShapeDtypeStruct(magnetic.shape, F32),
            in_specs=[anywhere] * 5 + [in_vmem] * 3,
            out_specs=anywhere,
            scratch_shapes=[
                pltpu.SMEM((lat_total,), jnp.int32),
                pltpu.SMEM((2 * lat_total,), F32),
                pltpu.SMEM((128,), F32),
                pltpu.VMEM((2, 2 * PADR + RAD * BAND, SEG), F32),
                pltpu.VMEM((2, RAD + 6, BAND + 16, SEG), F32),
                pltpu.VMEM((BAND, ROWS, SEG), F32),
                pltpu.VMEM((HALF, AZ, ROWS, SEG), F32),
                pltpu.VMEM((HALF, 8, 2 * SEG, 2 * SEG), BF16),
                pltpu.VMEM((HALF, 8, 2 * SEG, 2 * SEG), BF16),
                pltpu.VMEM((16 * ROWS, 2 * SEG), BF16),
                pltpu.VMEM((16 * ROWS, 2 * SEG), BF16),
                pltpu.VMEM((8 * ROWS, 2 * SEG), F32),
                pltpu.VMEM((HALF, AZ, ROWS, SEG), F32),
                pltpu.VMEM((BAND * ROWS, SEG), F32),
                pltpu.VMEM((3, RAD, BAND, SEG), F32),
                pltpu.VMEM((BAND, SEG), F32),
                pltpu.VMEM((HALF, AZ, SEG), F32),
                dma((3,)),
                dma((3,)),
                dma((HALF, AZ)),
                dma((HALF, AZ)),
                dma((HALF, AZ)),
                dma((HALF, AZ)),
                dma((2,)),
                dma((2,)),
                dma((3,)),
            ],
            compiler_params=pltpu.CompilerParams(
                collective_id=0, has_side_effects=True, vmem_limit_bytes=40 * 1024 * 1024
            ),
        )(
            magnetic, flat, kept_modes, jnp.asarray(lat_scalars), jnp.asarray(rad_scalars),
            jnp.asarray(first), jnp.asarray(second), jnp.asarray(third),
        )

    return jax.shard_map(
        on_device,
        mesh=mesh,
        in_specs=(P(None, None, "lat", "azim"), P()),
        out_specs=P(None, None, "lat", "azim"),
        check_vma=False,
    )
```

profile of v0, /device:TPU:1, one launch (start us, length us, event | category | flops | bytes accessed | tf_op | source)
XLA Modules:
  0.0 78.5 jit_solution(9369407637454996337)
XLA Ops:
  0.0 0.0 copy-start
  0.0 1.4 %copy-done = f32[3,32,32,128]{3,2,1,0:T(8,128)S(1)} copy-done((f32[3,32,32,128]{3,2,1,0:T(8,128)S(1)}, f32[3,32,32,128]{3,2,1,0:T(8,128)}, u32[]{:S(2)}) %copy-start) | copy-done | bytes 1572888
  1.4 0.0 copy-start.1
  1.4 0.9 %copy-done.1 = f32[128,256]{1,0:T(8,128)S(1)} copy-done((f32[128,256]{1,0:T(8,128)S(1)}, f32[128,256]{1,0:T(8,128)}, u32[]{:S(2)}) %copy-start.1) | copy-done | bytes 131096
  2.3 0.0 copy-start.2
  2.3 0.8 copy-done.2
  3.1 0.0 copy-start.3
  3.1 0.7 copy-done.3
  3.8 0.0 copy-start.4
  3.8 0.7 copy-done.4
  4.5 0.0 copy-start.5
  4.5 0.7 copy-done.5
  5.2 0.0 copy-start.6
  5.2 0.7 copy-done.6
  5.9 71.5 %shard_map.73 = f32[3,32,32,128]{3,2,1,0:T(8,128)S(1)} custom-call(f32[3,32,32,128]{3,2,1,0:T(8,128)S(1)} %copy-done, f32[3,1024,128]{2,1,0:T(8,128)S(1)} %bitcast.1, s32[2048]{0:T(1024)S(1)} %copy-done.5, f32[4096]{0:T(1024)S(1)} %copy-done.4, f32[128]{0:T(128)S(1)} %copy-done.6, f32[128,256]{1,0:T(8,128)S(1)} %copy-done.1, f32[2,32,128]{2,1,0:T(8,128)S(1)} %copy-done.2, ...), custom_call_target="tpu_custom_call" | custom-call | tf_op jit(solution)/shard_map/pallas_call | solution.py:315
  77.4 1.1 %copy.9 = f32[3,32,32,128]{3,2,1,0:T(8,128)} copy(f32[3,32,32,128]{3,2,1,0:T(8,128)S(1)} %shard_map.73) | data formatting | bytes 3145728
Async XLA Ops:
  0.0 1.4 %copy-start = (f32[3,32,32,128]{3,2,1,0:T(8,128)S(1)}, f32[3,32,32,128]{3,2,1,0:T(8,128)}, u32[]{:S(2)}) copy-start(f32[3,32,32,128]{3,2,1,0:T(8,128)} %x4.1) | copy-start | bytes 4718596
  1.4 0.9 %copy-start.1 = (f32[128,256]{1,0:T(8,128)S(1)}, f32[128,256]{1,0:T(8,128)}, u32[]{:S(2)}) copy-start(f32[128,256]{1,0:T(8,128)} %constant.12.clone.tab1) | copy-start | bytes 393220
  2.3 0.8 copy-start.2
  3.1 0.7 copy-start.3
  3.8 0.7 copy-start.4
  4.5 0.7 copy-start.5
  5.2 0.7 copy-start.6
where the time goes:
time: 78.9 us; the launch traced here: 78.5 us
  Pallas kernels  71.5 us (91%)
  local copies, waits for them, and re-layouts  7 us (9%)
    pallas_call x1, Pallas kernels, on_device(): pl.pallas_call(functools.partial(kernel, lat_total), out_shape=jax.ShapeD...  71.5 us
    unnamed x15, local copies, waits for them, and re-layouts  7 us

commit v1 on v0

--- a/solution.py
+++ b/solution.py
@@ -56,10 +56,10 @@
 
 def kernel(
     lat_total,
-    x4, x3, kept_hbm, latsc_hbm, radsc_hbm, tab1, tab2, tab3,
-    out,
-    kept, latsc, radsc, xs, ext, xt, rcv, whi, wlo, fhi, flo, acc, ret, az, outv, cot, gen,
-    in_sem, small_sem, fsend, frecv, rsend, rrecv, hsend, hrecv, out_sem,
+    x4, x3, kept_hbm, latsc_hbm, radsc_hbm, tab1_hbm, tab2_hbm, tab3_hbm,
+    outv,
+    kept, latsc, radsc, tab1, tab2, tab3, xs, ext, xt, rcv, whi, wlo, fhi, flo, acc, ret, az, cot, gen,
+    in_sem, small_sem, fsend, frecv, rsend, rrecv, hsend, hrecv,
 ):
     lat = lax.axis_index("lat")
     me = lax.axis_index("azim")
@@ -78,6 +78,9 @@
         pltpu.make_async_copy(kept_hbm, kept, small_sem.at[0]),
         pltpu.make_async_copy(latsc_hbm, latsc, small_sem.at[1]),
         pltpu.make_async_copy(radsc_hbm, radsc, small_sem.at[2]),
+        pltpu.make_async_copy(tab1_hbm, tab1, small_sem.at[3]),
+        pltpu.make_async_copy(tab2_hbm, tab2, small_sem.at[4]),
+        pltpu.make_async_copy(tab3_hbm, tab3, small_sem.at[5]),
     ]
     for copy in loads + smalls:
         copy.start()
@@ -276,23 +279,15 @@
             return carry
 
         lax.fori_loop(0, RAD, combine, 0)
-        where = (slice(0, 2), slice(None), slice(AZ * half, AZ * half + AZ), slice(None))
-        copy = pltpu.make_async_copy(outv.at[where], out.at[where], out_sem.at[half])
-        copy.start()
-        return copy
 
     lax.fori_loop(0, RAD, stencils, 0)
-    written = [pltpu.make_async_copy(outv.at[2], out.at[2], out_sem.at[2])]
-    written[0].start()
     back = []
     for half in range(HALF):
         back += convert_and_apply(half)
     for half in range(HALF):
-        written.append(finish(half))
+        finish(half)
     for copy in forward + back + halos:
         copy.wait_send()
-    for copy in written:
-        copy.wait()
 
 
 def solution(mesh):
@@ -309,18 +304,20 @@
 
     def on_device(magnetic, kept_modes):
         flat = magnetic.reshape(3, RAD * BAND, SEG)
-        anywhere = pl.BlockSpec(memory_space=pl.ANY)
-        in_vmem = pl.BlockSpec(memory_space=pltpu.VMEM)
+        in_hbm = pl.BlockSpec(memory_space=pltpu.HBM)
         dma = pltpu.SemaphoreType.DMA
         return pl.pallas_call(
             functools.partial(kernel, lat_total),
             out_shape=jax.ShapeDtypeStruct(magnetic.shape, F32),
-            in_specs=[anywhere] * 5 + [in_vmem] * 3,
-            out_specs=anywhere,
+            in_specs=[in_hbm] * 8,
+            out_specs=pl.BlockSpec(memory_space=pltpu.VMEM),
             scratch_shapes=[
                 pltpu.SMEM((lat_total,), jnp.int32),
                 pltpu.SMEM((2 * lat_total,), F32),
                 pltpu.SMEM((128,), F32),
+                pltpu.VMEM(first.shape, F32),
+                pltpu.VMEM(second.shape, F32),
+                pltpu.VMEM(third.shape, F32),
                 pltpu.VMEM((2, 2 * PADR + RAD * BAND, SEG), F32),
                 pltpu.VMEM((2, RAD + 6, BAND + 16, SEG), F32),
                 pltpu.VMEM((BAND, ROWS, SEG), F32),
@@ -332,26 +329,25 @@
                 pltpu.VMEM((8 * ROWS, 2 * SEG), F32),
                 pltpu.VMEM((HALF, AZ, ROWS, SEG), F32),
                 pltpu.VMEM((BAND * ROWS, SEG), F32),
-                pltpu.VMEM((3, RAD, BAND, SEG), F32),
                 pltpu.VMEM((BAND, SEG), F32),
                 pltpu.VMEM((HALF, AZ, SEG), F32),
                 dma((3,)),
-                dma((3,)),
+                dma((6,)),
                 dma((HALF, AZ)),
                 dma((HALF, AZ)),
                 dma((HALF, AZ)),
                 dma((HALF, AZ)),
                 dma((2,)),
                 dma((2,)),
-                dma((3,)),
             ],
             compiler_params=pltpu.CompilerParams(
                 collective_id=0, has_side_effects=True, vmem_limit_bytes=40 * 1024 * 1024
             ),
         )(
+            *(pltpu.with_memory_space_constraint(v, pltpu.HBM) for v in (
             magnetic, flat, kept_modes, jnp.asarray(lat_scalars), jnp.asarray(rad_scalars),
             jnp.asarray(first), jnp.asarray(second), jnp.asarray(third),
-        )
+        )))
 
     return jax.shard_map(
         on_device,

time: 78.9 us -> 72.6 us (0.920)
  local copies, waits for them, and re-layouts: 7 us -> 1.15 us
    unnamed x15 -> x1, local copies, waits for them, and re-layouts: 7 us -> 1.15 us
where the time goes in v1:
time: 72.6 us; the launch traced here: 72.4 us
  Pallas kernels  71.3 us (98%)
  local copies, waits for them, and re-layouts  1.15 us (2%)
    pallas_call x1, Pallas kernels, on_device(): pl.pallas_call(functools.partial(kernel, lat_total), out_shape=jax.ShapeD...  71.3 us

profile of v1, /device:TPU:1, one launch (start us, length us, event | category | flops | bytes accessed | tf_op | source)
XLA Modules:
  0.0 72.4 jit_solution(9176384081999270852)
XLA Ops:
  0.0 71.3 %shard_map.73 = f32[3,32,32,128]{3,2,1,0:T(8,128)S(1)} custom-call(f32[3,32,32,128]{3,2,1,0:T(8,128)} %x4.1, f32[3,1024,128]{2,1,0:T(8,128)} %bitcast.1, s32[2048]{0:T(1024)} %kept_hbm.1, f32[4096]{0:T(1024)} %constant.10.clone.latsc_hbm, f32[128]{0:T(128)} %constant.11.clone.radsc_hbm, f32[128,256]{1,0:T(8,128)} %constant.12.clone.tab1_hbm, ...), custom_call_target="tpu_custom_call" | custom-call | tf_op jit(solution)/shard_map/pallas_call | solution.py:309
  71.3 1.1 %copy.9 = f32[3,32,32,128]{3,2,1,0:T(8,128)} copy(f32[3,32,32,128]{3,2,1,0:T(8,128)S(1)} %shard_map.73) | data formatting | bytes 3145728

commit v2 on v1

--- a/solution.py
+++ b/solution.py
@@ -58,8 +58,8 @@
     lat_total,
     x4, x3, kept_hbm, latsc_hbm, radsc_hbm, tab1_hbm, tab2_hbm, tab3_hbm,
     outv,
-    kept, latsc, radsc, tab1, tab2, tab3, xs, ext, xt, rcv, whi, wlo, fhi, flo, acc, ret, az, cot, gen,
-    in_sem, small_sem, fsend, frecv, rsend, rrecv, hsend, hrecv,
+    kept, latsc, radsc, tab1, tab2, tab3, xs, ext, edge, beyond, xt, rcv, whi, wlo, fhi, flo, acc, ret, az, cot, gen,
+    in_sem, small_sem, fsend, frecv, rsend, rrecv, hsend, hrecv, joined,
 ):
     lat = lax.axis_index("lat")
     me = lax.axis_index("azim")
@@ -70,9 +70,10 @@
     south = (lat + 1) % lats
 
     loads = [
-        pltpu.make_async_copy(x3.at[0:2], xs.at[:, PADR : PADR + RAD * BAND, :], in_sem.at[0]),
+        pltpu.make_async_copy(x3.at[0:2], xs.at[0:2, PADR : PADR + RAD * BAND, :], in_sem.at[0]),
         pltpu.make_async_copy(x4.at[0], ext.at[0, 3 : 3 + RAD, 8 : 8 + BAND, :], in_sem.at[1]),
         pltpu.make_async_copy(x4.at[2], ext.at[1, 3 : 3 + RAD, 8 : 8 + BAND, :], in_sem.at[2]),
+        pltpu.make_async_copy(x3.at[2], xs.at[2, PADR : PADR + RAD * BAND, :], in_sem.at[3]),
     ]
     smalls = [
         pltpu.make_async_copy(kept_hbm, kept, small_sem.at[0]),
@@ -86,19 +87,46 @@
         copy.start()
 
     barrier = pltpu.get_barrier_semaphore()
-    for step in range(1, AZ):
-        pl.semaphore_signal(barrier, inc=1, device_id={"azim": (me + step) % AZ}, device_id_type=MESH)
-    pl.semaphore_signal(barrier, inc=1, device_id={"lat": north}, device_id_type=MESH)
-    pl.semaphore_signal(barrier, inc=1, device_id={"lat": south}, device_id_type=MESH)
+
+    @pl.when(me != 0)
+    def _():
+        for step in range(1, AZ):
+            pl.semaphore_signal(barrier, inc=1, device_id={"azim": (me + step) % AZ}, device_id_type=MESH)
+
+    @pl.when(lat > 0)
+    def _():
+        pl.semaphore_signal(barrier, inc=1, device_id={"lat": north}, device_id_type=MESH)
+
+    @pl.when(lat < lats - 1)
+    def _():
+        pl.semaphore_signal(barrier, inc=1, device_id={"lat": south}, device_id_type=MESH)
+
+    bands_beside = (lat + lats - 1) // lats + 1 - (lat + 1) // lats
+    pl.semaphore_wait(barrier, AZ - 1 - (me + AZ - 1) // AZ + bands_beside)
+
+    @pl.when(me == 0)
+    def _():
+        for step in range(1, AZ):
+            pl.semaphore_signal(joined, inc=1, device_id={"azim": step}, device_id_type=MESH)
+
     loads[0].wait()
-    pl.semaphore_wait(barrier, AZ + 1)
 
     peers = []
     for chips, flip in send_order():
         peer = ((chip + chips + 8) % 8) * 2 + (core + flip) % 2
         peers.append((peer, chips == 0 and flip == 0))
-    forward = []
-    for half in range(HALF):
+    def send_rows(half, row, peer):
+        return pltpu.make_async_remote_copy(
+            src_ref=xt.at[row],
+            dst_ref=rcv.at[half, me],
+            send_sem=fsend.at[half, peer],
+            recv_sem=frecv.at[half, me],
+            device_id={"azim": peer},
+            device_id_type=MESH,
+        )
+
+    def forward_half(half, all_joined):
+        sent = []
         for peer, own in peers:
             row = peer + AZ * half
             for c in range(2):
@@ -109,39 +137,16 @@
             if own:
                 pltpu.make_async_copy(xt.at[row], rcv.at[half, me], frecv.at[half, me]).start()
             else:
-                copy = pltpu.make_async_remote_copy(
-                    src_ref=xt.at[row],
-                    dst_ref=rcv.at[half, me],
-                    send_sem=fsend.at[half, peer],
-                    recv_sem=frecv.at[half, me],
-                    device_id={"azim": peer},
-                    device_id_type=MESH,
-                )
-                copy.start()
-                forward.append(copy)
-
-    loads[1].wait()
-    loads[2].wait()
-    halos = [
-        pltpu.make_async_remote_copy(
-            src_ref=ext.at[:, 3 : 3 + RAD, BAND : BAND + 8, :],
-            dst_ref=ext.at[:, 3 : 3 + RAD, 0:8, :],
-            send_sem=hsend.at[0],
-            recv_sem=hrecv.at[0],
-            device_id={"lat": south},
-            device_id_type=MESH,
-        ),
-        pltpu.make_async_remote_copy(
-            src_ref=ext.at[:, 3 : 3 + RAD, 8:16, :],
-            dst_ref=ext.at[:, 3 : 3 + RAD, 8 + BAND : 16 + BAND, :],
-            send_sem=hsend.at[1],
-            recv_sem=hrecv.at[1],
-            device_id={"lat": north},
-            device_id_type=MESH,
-        ),
-    ]
-    for copy in halos:
-        copy.start()
+                copy = send_rows(half, row, peer)
+                if all_joined:
+                    copy.start()
+                else:
+                    pl.when(peer != 0)(copy.start)
+                sent.append(copy)
+        return sent
+
+    forward = forward_half(0, False)
+
     for copy in smalls:
         copy.wait()
 
@@ -181,6 +186,46 @@
                             whi[at] = high
                             wlo[at] = low
 
+    @pl.when(me != 0)
+    def _():
+        pl.semaphore_wait(joined, 1)
+        send_rows(0, 0, 0).start()
+
+    forward += forward_half(1, True)
+
+    loads[3].wait()
+    for side, first_row in ((0, BAND - 3), (1, 0)):
+        for i in range(3):
+            for c in range(2):
+                for k in range(RAD // 8):
+                    edge[side, c, i, 8 * k : 8 * k + 8, :] = xs[
+                        2 * c, pl.ds(PADR + 8 * k * BAND + first_row + i, 8, stride=BAND), :
+                    ]
+    halos = [
+        pltpu.make_async_remote_copy(
+            src_ref=edge.at[side],
+            dst_ref=beyond.at[side],
+            send_sem=hsend.at[side],
+            recv_sem=hrecv.at[side],
+            device_id={"lat": (south, north)[side]},
+            device_id_type=MESH,
+        )
+        for side in range(2)
+    ]
+    pl.when(lat < lats - 1)(halos[0].start)
+    pl.when(lat > 0)(halos[1].start)
+
+    @pl.when(lat == 0)
+    def _():
+        beyond[0] = jnp.zeros((2, 3, RAD, SEG), F32)
+
+    @pl.when(lat == lats - 1)
+    def _():
+        beyond[1] = jnp.zeros((2, 3, RAD, SEG), F32)
+
+    loads[1].wait()
+    loads[2].wait()
+
     zeros = jnp.zeros((3, BAND, SEG), F32)
     ext[1, 0:3, 8 : 8 + BAND, :] = zeros
     ext[1, 3 + RAD : 6 + RAD, 8 : 8 + BAND, :] = zeros
@@ -188,15 +233,12 @@
     xs[1, PADR + RAD * BAND : 2 * PADR + RAD * BAND, :] = jnp.zeros((PADR, SEG), F32)
     for t in range(BAND):
         cot[t : t + 1, :] = jnp.full((1, SEG), latsc[lat_total + lat * BAND + t], F32)
-    for copy in halos:
-        copy.wait_recv()
 
     def stencils(r, carry):
         for c in range(2):
-            top = ext[c, r + 3, 0:8, :]
-            ext[c, r + 3, 0:8, :] = jnp.where(lat == 0, jnp.zeros_like(top), top)
-            end = ext[c, r + 3, 8 + BAND : 16 + BAND, :]
-            ext[c, r + 3, 8 + BAND : 16 + BAND, :] = jnp.where(lat == lats - 1, jnp.zeros_like(end), end)
+            for i in range(3):
+                ext[c, r + 3, 5 + i : 6 + i, :] = beyond[0, c, i, pl.ds(r, 1), :]
+                ext[c, r + 3, 8 + BAND + i : 9 + BAND + i, :] = beyond[1, c, i, pl.ds(r, 1), :]
         inverse = radsc[64 + r]
         th_r = jnp.zeros((BAND, SEG), F32)
         th_p = jnp.zeros((BAND, SEG), F32)
@@ -280,14 +322,18 @@
 
         lax.fori_loop(0, RAD, combine, 0)
 
-    lax.fori_loop(0, RAD, stencils, 0)
     back = []
     for half in range(HALF):
         back += convert_and_apply(half)
+    pl.when(lat > 0)(halos[0].wait_recv)
+    pl.when(lat < lats - 1)(halos[1].wait_recv)
+    lax.fori_loop(0, RAD, stencils, 0)
     for half in range(HALF):
         finish(half)
-    for copy in forward + back + halos:
+    for copy in forward + back:
         copy.wait_send()
+    pl.when(lat < lats - 1)(halos[0].wait_send)
+    pl.when(lat > 0)(halos[1].wait_send)
 
 
 def solution(mesh):
@@ -318,8 +364,10 @@
                 pltpu.VMEM(first.shape, F32),
                 pltpu.VMEM(second.shape, F32),
                 pltpu.VMEM(third.shape, F32),
-                pltpu.VMEM((2, 2 * PADR + RAD * BAND, SEG), F32),
+                pltpu.VMEM((3, 2 * PADR + RAD * BAND, SEG), F32),
                 pltpu.VMEM((2, RAD + 6, BAND + 16, SEG), F32),
+                pltpu.VMEM((2, 2, 3, RAD, SEG), F32),
+                pltpu.VMEM((2, 2, 3, RAD, SEG), F32),
                 pltpu.VMEM((BAND, ROWS, SEG), F32),
                 pltpu.VMEM((HALF, AZ, ROWS, SEG), F32),
                 pltpu.VMEM((HALF, 8, 2 * SEG, 2 * SEG), BF16),
@@ -331,7 +379,7 @@
                 pltpu.VMEM((BAND * ROWS, SEG), F32),
                 pltpu.VMEM((BAND, SEG), F32),
                 pltpu.VMEM((HALF, AZ, SEG), F32),
-                dma((3,)),
+                dma((4,)),
                 dma((6,)),
                 dma((HALF, AZ)),
                 dma((HALF, AZ)),
@@ -339,6 +387,7 @@
                 dma((HALF, AZ)),
                 dma((2,)),
                 dma((2,)),
+                pltpu.SemaphoreType.REGULAR,
             ],
             compiler_params=pltpu.CompilerParams(
                 collective_id=0, has_side_effects=True, vmem_limit_bytes=40 * 1024 * 1024

time: 72.6 us -> 58.1 us (0.80)
  Pallas kernels: 71.3 us -> 56.8 us
    pallas_call x1, Pallas kernels: 71.3 us -> 56.8 us  [on_device(): pl.pallas_call(functools.partial(kernel, lat_total), out_shape=jax.ShapeD...]
where the time goes in v2:
time: 58.1 us; the launch traced here: 58 us
  Pallas kernels  56.8 us (98%)
  local copies, waits for them, and re-layouts  1.15 us (2%)
    pallas_call x1, Pallas kernels, on_device(): pl.pallas_call(functools.partial(kernel, lat_total), out_shape=jax.ShapeD...  56.8 us

profile of v2, /device:TPU:1, one launch (start us, length us, event | category | flops | bytes accessed | tf_op | source)
XLA Modules:
  0.0 58.0 jit_solution(14054728923581724225)
XLA Ops:
  0.0 56.8 %shard_map.73 = f32[3,32,32,128]{3,2,1,0:T(8,128)S(1)} custom-call(f32[3,32,32,128]{3,2,1,0:T(8,128)} %x4.1, f32[3,1024,128]{2,1,0:T(8,128)} %bitcast.1, s32[2048]{0:T(1024)} %kept_hbm.1, f32[4096]{0:T(1024)} %constant.10.clone.latsc_hbm, f32[128]{0:T(128)} %constant.11.clone.radsc_hbm, f32[128,256]{1,0:T(8,128)} %constant.12.clone.tab1_hbm, ...), custom_call_target="tpu_custom_call" | custom-call | tf_op jit(solution)/shard_map/pallas_call | solution.py:355
  56.8 1.1 %copy.9 = f32[3,32,32,128]{3,2,1,0:T(8,128)} copy(f32[3,32,32,128]{3,2,1,0:T(8,128)S(1)} %shard_map.73) | data formatting | bytes 3145728

commit v3 on v2

--- a/solution.py
+++ b/solution.py
@@ -46,10 +46,14 @@
     return high, (value - high.astype(F32)).astype(BF16)
 
 
+def is_zero(value, bound):
+    return 1 - (value + bound - 1) // bound
+
+
 def send_order():
     order = []
-    for chips in (4, 3, -3, 2, -2, 1, -1, 0):
-        for core in (0, 1):
+    for chips in (0, 1, -1, 2, -2, 3, -3, 4):
+        for core in (1, 0):
             order.append((chips, core))
     return order
 
@@ -59,7 +63,7 @@
     x4, x3, kept_hbm, latsc_hbm, radsc_hbm, tab1_hbm, tab2_hbm, tab3_hbm,
     outv,
     kept, latsc, radsc, tab1, tab2, tab3, xs, ext, edge, beyond, xt, rcv, whi, wlo, fhi, flo, acc, ret, az, cot, gen,
-    in_sem, small_sem, fsend, frecv, rsend, rrecv, hsend, hrecv, joined,
+    in_sem, small_sem, fsend, frecv, rsend, rrecv, hsend, hrecv, joined, beside,
 ):
     lat = lax.axis_index("lat")
     me = lax.axis_index("azim")
@@ -83,8 +87,7 @@
         pltpu.make_async_copy(tab2_hbm, tab2, small_sem.at[4]),
         pltpu.make_async_copy(tab3_hbm, tab3, small_sem.at[5]),
     ]
-    for copy in loads + smalls:
-        copy.start()
+    loads[0].start()
 
     barrier = pltpu.get_barrier_semaphore()
 
@@ -93,16 +96,36 @@
         for step in range(1, AZ):
             pl.semaphore_signal(barrier, inc=1, device_id={"azim": (me + step) % AZ}, device_id_type=MESH)
 
-    @pl.when(lat > 0)
+    greet_south = ((lat + 1) % 4 + 3) // 4 - is_zero(me, AZ) * is_zero(lat, lats)
+    heard_north = (lat % 4 + 3) // 4 - is_zero(me, AZ) * is_zero((lat + lats - 1) % lats, lats)
+    has_south = 1 - is_zero(lats - 1 - lat, lats)
+    has_north = 1 - is_zero(lat, lats)
+    greets_south = has_south * greet_south == 1
+    waits_south = has_south * (1 - greet_south) == 1
+    greets_north = has_north * (1 - heard_north) == 1
+    waits_north = has_north * heard_north == 1
+
+    @pl.when(greets_north)
     def _():
         pl.semaphore_signal(barrier, inc=1, device_id={"lat": north}, device_id_type=MESH)
 
-    @pl.when(lat < lats - 1)
+    @pl.when(greets_south)
     def _():
         pl.semaphore_signal(barrier, inc=1, device_id={"lat": south}, device_id_type=MESH)
 
-    bands_beside = (lat + lats - 1) // lats + 1 - (lat + 1) // lats
-    pl.semaphore_wait(barrier, AZ - 1 - (me + AZ - 1) // AZ + bands_beside)
+    for copy in loads[1:] + smalls:
+        copy.start()
+    pl.semaphore_wait(
+        barrier, AZ - 1 - (me + AZ - 1) // AZ + has_south * (1 - greet_south) + has_north * heard_north
+    )
+
+    @pl.when(waits_north)
+    def _():
+        pl.semaphore_signal(beside.at[0], inc=1, device_id={"lat": north}, device_id_type=MESH)
+
+    @pl.when(waits_south)
+    def _():
+        pl.semaphore_signal(beside.at[1], inc=1, device_id={"lat": south}, device_id_type=MESH)
 
     @pl.when(me == 0)
     def _():
@@ -125,27 +148,25 @@
             device_id_type=MESH,
         )
 
-    def forward_half(half, all_joined):
-        sent = []
-        for peer, own in peers:
-            row = peer + AZ * half
-            for c in range(2):
-                for k in range(RAD // 8):
-                    xt[row, c * RAD + 8 * k : c * RAD + 8 * k + 8, :] = xs[
-                        c, pl.ds(PADR + 8 * k * BAND + row, 8, stride=BAND), :
-                    ]
-            if own:
-                pltpu.make_async_copy(xt.at[row], rcv.at[half, me], frecv.at[half, me]).start()
-            else:
-                copy = send_rows(half, row, peer)
-                if all_joined:
-                    copy.start()
-                else:
-                    pl.when(peer != 0)(copy.start)
-                sent.append(copy)
-        return sent
-
-    forward = forward_half(0, False)
+    def fill(half, peer):
+        row = peer + AZ * half
+        for c in range(2):
+            for k in range(RAD // 8):
+                xt[row, c * RAD + 8 * k : c * RAD + 8 * k + 8, :] = xs[
+                    c, pl.ds(PADR + 8 * k * BAND + row, 8, stride=BAND), :
+                ]
+
+    others = [peer for peer, own in peers if not own]
+    forward = []
+    for half in range(HALF):
+        for peer in others:
+            fill(half, peer)
+            copy = send_rows(half, peer + AZ * half, peer)
+            if half == 0:
+                pl.when(peer != 0)(copy.start)
+            forward.append(copy)
+        fill(half, me)
+        pltpu.make_async_copy(xt.at[me + AZ * half], rcv.at[half, me], frecv.at[half, me]).start()
 
     for copy in smalls:
         copy.wait()
@@ -191,7 +212,8 @@
         pl.semaphore_wait(joined, 1)
         send_rows(0, 0, 0).start()
 
-    forward += forward_half(1, True)
+    for peer in others:
+        send_rows(1, peer + AZ, peer).start()
 
     loads[3].wait()
     for side, first_row in ((0, BAND - 3), (1, 0)):
@@ -212,7 +234,17 @@
         )
         for side in range(2)
     ]
+
+    @pl.when(greets_south)
+    def _():
+        pl.semaphore_wait(beside.at[0], 1)
+
     pl.when(lat < lats - 1)(halos[0].start)
+
+    @pl.when(greets_north)
+    def _():
+        pl.semaphore_wait(beside.at[1], 1)
+
     pl.when(lat > 0)(halos[1].start)
 
     @pl.when(lat == 0)
@@ -299,8 +331,21 @@
                     device_id={"azim": peer},
                     device_id_type=MESH,
                 )
-                copy.start()
+                if half == 0:
+                    copy.start()
                 sent.append(copy)
+        if half == HALF - 1:
+            for target_chip in (0, 1, 7, 2, 6, 3, 5, 4):
+                for peer in (2 * target_chip, 2 * target_chip + 1):
+                    copy = pltpu.make_async_remote_copy(
+                        src_ref=ret.at[half, peer],
+                        dst_ref=az.at[pl.ds(pl.multiple_of((me + AZ * half) * ROWS, ROWS), ROWS), :],
+                        send_sem=rsend.at[half, peer],
+                        recv_sem=rrecv.at[half, me],
+                        device_id={"azim": peer},
+                        device_id_type=MESH,
+                    )
+                    pl.when(me != peer)(copy.start)
         return sent
 
     def finish(half):
@@ -388,6 +433,7 @@
                 dma((2,)),
                 dma((2,)),
                 pltpu.SemaphoreType.REGULAR,
+                pltpu.SemaphoreType.REGULAR((2,)),
             ],
             compiler_params=pltpu.CompilerParams(
                 collective_id=0, has_side_effects=True, vmem_limit_bytes=40 * 1024 * 1024

time: 58.1 us -> 57.5 us (0.990)
  the two profiles are of different devices: /device:TPU:1 before, /device:TPU:17 now
where the time goes in v3:
time: 57.5 us; the launch traced here: 57.3 us
  Pallas kernels  56.2 us (98%)
  local copies, waits for them, and re-layouts  1.15 us (2%)
    pallas_call x1, Pallas kernels, on_device(): pl.pallas_call(functools.partial(kernel, lat_total), out_shape=jax.ShapeD...  56.2 us

profile of v3, /device:TPU:17, one launch (start us, length us, event | category | flops | bytes accessed | tf_op | source)
XLA Modules:
  0.0 57.3 jit_solution(10023787061911836459)
XLA Ops:
  0.0 56.2 %shard_map.73 = f32[3,32,32,128]{3,2,1,0:T(8,128)S(1)} custom-call(f32[3,32,32,128]{3,2,1,0:T(8,128)} %x4.1, f32[3,1024,128]{2,1,0:T(8,128)} %bitcast.1, s32[2048]{0:T(1024)} %kept_hbm.1, f32[4096]{0:T(1024)} %constant.10.clone.latsc_hbm, f32[128]{0:T(128)} %constant.11.clone.radsc_hbm, f32[128,256]{1,0:T(8,128)} %constant.12.clone.tab1_hbm, ...), custom_call_target="tpu_custom_call" | custom-call | tf_op jit(solution)/shard_map/pallas_call | solution.py:400
  56.2 1.1 %copy.9 = f32[3,32,32,128]{3,2,1,0:T(8,128)} copy(f32[3,32,32,128]{3,2,1,0:T(8,128)S(1)} %shard_map.73) | data formatting | bytes 3145728
